TPU v7x, 32 devices: a whole 2x2x4 slice. The times are simulated.
32 devices in a mesh: site: 2 (over y), pts: 4 (over z), var: 2 (over x), cmp: 2 (over core).
Axes of the slice: x: 2, y: 2, z: 4, core: 2. Of those that a mesh axis runs over, the one named last changes fastest.
Arguments:
- sgt: bfloat16 [6, 3, 128, 4096], P('cmp', None, ('site', 'pts')), parts along dimension 2, may hold values from -6 to 6
- moment: float32 [6, 64], P('cmp', ('site', 'pts')), parts along dimension 1, may hold values from -6 to 6
- slip_spec: float32 [16, 2, 4096], replicated, may hold values from -3 to 3
- rp_slab: int32 [64], P('site'), parts along dimension 0, may hold values from 0 to 63, as said below
- rup_counts: int32 [8, 6], P(('site', 'pts')), parts along dimension 0, may hold values from 1 to 2, 8 in all within a row
- var_rupture: int32 [32], P('site'), parts along dimension 0, may hold values from 0 to 5
- var_source: int32 [32, 2], P('site'), parts along dimension 0, may hold values from 0 to 15
- owner_map: int32 [32], P('site'), parts along dimension 0, may hold values from 0 to 15, each once
Outputs:
- seismograms: float32 [32, 3, 4096], P(('site', 'pts', 'var', 'cmp')), parts along dimension 0
There are 2 independent parts, one for each index of `site`. A program takes and returns all parts, laid end to end along the dimension named above; an argument that names none is the same for every part. Nothing has to cross between parts.
Inputs may be any that keep to these rules, and one draw needn't show every extreme that they name: `rp_slab`: in each aligned block of 8 rupture-points (one owner's), at most 4 name slab points of one reader (slab points k * 16 to (k + 1) * 16 - 1 belong to reader k), and in every block some reader is named exactly 4 times. `rup_counts`: each row gives, for the ruptures in order, how many of that owner's 8 slots belong to each; every rupture has 1 or more on every owner, the row sums to 8, and some entry of each row is exactly 2. `owner_map`: A permutation of the variations.
All inputs are finite; a program needn't handle non-finite values.
Results may differ from a plain program's by a relative error of at most 0.0003.
Values may be sent and summed in bfloat16 or wider, within the bound.
No kernel may reach another device: no remote copies, remote signals or barrier semaphores. Data moves between devices by JAX's collectives and lax.ppermute only.
A program may use at most 64 MiB of HBM per device.

v0:
```python
import math

import jax
import jax.numpy as jnp
from jax import lax
from jax.sharding import PartitionSpec as P

TAU = 4


highest = lax.Precision.HIGHEST


def cos_sin(numerator, period):
    angles = numerator.astype(jnp.float32) * (2.0 * math.pi / period)
    return (jnp.cos(angles), jnp.sin(angles))


def forward_spectra(signal):
    series, samples = signal.shape
    length = 2 * samples
    blocks = length // 128
    rows_half = blocks // 2
    row_iota = jnp.arange(rows_half, dtype=jnp.int32)
    outer_iota = jnp.arange(blocks, dtype=jnp.int32)
    lane_iota = jnp.arange(128, dtype=jnp.int32)
    half_iota = jnp.arange(64, dtype=jnp.int32)
    first_cos, first_sin = cos_sin(row_iota[:, None] * outer_iota[None, :] % blocks, blocks)
    first_table = jnp.concatenate([first_cos, -first_sin], axis=1)
    shaped = signal.reshape(series, rows_half, 128)
    first_pass = jnp.einsum("sab,am->smb", shaped, first_table, precision=highest)
    real_part = first_pass[:, :blocks]
    imag_part = first_pass[:, blocks:]
    turn_cos, turn_sin = cos_sin(outer_iota[:, None] * lane_iota[None, :], length)
    turned_real = real_part * turn_cos + imag_part * turn_sin
    turned_imag = imag_part * turn_cos - real_part * turn_sin
    second_cos, second_sin = cos_sin(lane_iota[:, None] * half_iota[None, :] % 128, 128)
    second_table = jnp.concatenate(
        [
            jnp.concatenate([second_cos, -second_sin], axis=1),
            jnp.concatenate([second_sin, second_cos], axis=1),
        ],
        axis=0,
    )
    joined = jnp.concatenate([turned_real, turned_imag], axis=-1)
    return jnp.einsum("skb,bm->skm", joined, second_table, precision=highest)


def inverse_series(spectra):
    series, blocks, lanes = spectra.shape
    samples = blocks * 64
    length = 2 * samples
    rows_half = blocks // 2
    outer_iota = jnp.arange(blocks, dtype=jnp.int32)
    lane_iota = jnp.arange(128, dtype=jnp.int32)
    half_iota = jnp.arange(64, dtype=jnp.int32)
    row_iota = jnp.arange(rows_half, dtype=jnp.int32)
    frequency = outer_iota[:, None] + blocks * half_iota[None, :]
    weights = jnp.where(frequency == 0, 1.0, 2.0).astype(jnp.float32) / length
    weights = jnp.concatenate([weights, weights], axis=-1)
    scaled = spectra * weights[None]
    third_cos, third_sin = cos_sin(half_iota[:, None] * lane_iota[None, :] % 128, 128)
    third_table = jnp.concatenate(
        [
            jnp.concatenate([third_cos, third_sin], axis=1),
            jnp.concatenate([-third_sin, third_cos], axis=1),
        ],
        axis=0,
    )
    middle = jnp.einsum("skm,mb->skb", scaled, third_table, precision=highest)
    mid_real = middle[..., :128]
    mid_imag = middle[..., 128:]
    turn_cos, turn_sin = cos_sin(outer_iota[:, None] * lane_iota[None, :], length)
    back_real = mid_real * turn_cos - mid_imag * turn_sin
    back_imag = mid_real * turn_sin + mid_imag * turn_cos
    stacked = jnp.concatenate([back_real, back_imag], axis=1)
    last_cos, last_sin = cos_sin(outer_iota[:, None] * row_iota[None, :] % blocks, blocks)
    last_table = jnp.concatenate([last_cos, -last_sin], axis=0)
    result = jnp.einsum("smb,ma->sab", stacked, last_table, precision=highest)
    return result.reshape(series, samples)


def per_device(sgt, moment, slip_spec, rp_slab, rup_counts, var_rupture, var_source, owner_map):
    comp_half, seis_comp, slab_dev, samples = sgt.shape
    rp_dev = moment.shape[1]
    owners = lax.axis_size("pts")
    my_owner = lax.axis_index("pts")
    var_count = lax.axis_size("var")
    my_var = lax.axis_index("var")
    cmp_count = lax.axis_size("cmp")
    my_core = lax.axis_index("cmp")
    capacity = max(2, (2 * rp_dev + owners - 1) // owners)
    length = 2 * samples
    blocks = length // 128
    readers = rp_slab // slab_dev
    within = rp_slab % slab_dev
    reader_rows = readers.reshape(owners, rp_dev)
    slot_iota = jnp.arange(rp_dev, dtype=jnp.int32)
    lower_slot = slot_iota[None, :] < slot_iota[:, None]
    same_reader = reader_rows[:, :, None] == reader_rows[:, None, :]
    ranks = jnp.sum(same_reader & lower_slot[None], axis=2)
    owner_ids = jnp.arange(owners, dtype=jnp.int32)[:, None]
    target = (owner_ids * capacity + ranks).reshape(-1)
    spill = owners * capacity
    place = jnp.where(readers == my_owner, target, spill)
    send_rows = jnp.zeros((spill,), jnp.int32).at[place].set(within, mode="drop")
    send_live = jnp.zeros((spill,), jnp.bool_).at[place].set(True, mode="drop")
    outgoing = jnp.take(sgt, send_rows, axis=2)
    outgoing = jnp.where(send_live[None, None, :, None], outgoing, jnp.zeros((), outgoing.dtype))
    received = lax.all_to_all(outgoing, "pts", split_axis=2, concat_axis=2, tiled=True)
    pick_rows = reader_rows[my_owner] * capacity + ranks[my_owner]
    picked = jnp.take(received, pick_rows, axis=2)
    partial_value = jnp.sum(moment[:, None, :, None] * picked.astype(jnp.float32), axis=0)
    pieces = lax.all_to_all(partial_value[None], "cmp", split_axis=2, concat_axis=0, tiled=True)
    half_sum = jnp.sum(pieces, axis=0)
    half_points = rp_dev // cmp_count
    half_spec = forward_spectra(half_sum.reshape(seis_comp * half_points, samples)).reshape(
        seis_comp, half_points, blocks, 128
    )
    spectra = lax.all_gather(half_spec, "cmp", axis=1, tiled=True)
    counts_all = lax.all_gather(rup_counts, "pts", axis=0, tiled=True)
    my_counts = rup_counts[0]
    ruptures = my_counts.shape[0]
    rupture_iota = jnp.arange(ruptures, dtype=jnp.int32)
    inclusive = jnp.cumsum(my_counts)
    rupture_of = jnp.sum(inclusive[None, :] <= slot_iota[:, None], axis=1)
    owner_mask = (jnp.arange(owners, dtype=jnp.int32) < my_owner)[:, None]
    before = jnp.sum(jnp.where(owner_mask, counts_all, 0), axis=0)
    lengths = jnp.sum(counts_all, axis=0)
    point_onehot = (rupture_of[:, None] == rupture_iota[None, :]).astype(jnp.int32)
    shift_table = before - inclusive + my_counts
    position = slot_iota + jnp.sum(point_onehot * shift_table[None, :], axis=1)
    outer_iota = jnp.arange(blocks, dtype=jnp.int32)
    half_iota = jnp.arange(64, dtype=jnp.int32)
    frequency = outer_iota[:, None] + blocks * half_iota[None, :]
    point_cos, point_sin = cos_sin(
        frequency[None] * (TAU * position)[:, None, None] % length, length
    )
    point_cos = point_cos[None]
    point_sin = point_sin[None]
    real_x = spectra[..., :64]
    imag_x = spectra[..., 64:]
    lagged = jnp.concatenate(
        [real_x * point_cos + imag_x * point_sin, imag_x * point_cos - real_x * point_sin], axis=-1
    )
    leading = jnp.concatenate(
        [real_x * point_cos - imag_x * point_sin, imag_x * point_cos + real_x * point_sin], axis=-1
    )
    per_owner = owner_map.shape[0] // (owners * var_count * cmp_count)
    row_owner = jnp.arange(owners, dtype=jnp.int32)[:, None]
    row_unit = jnp.arange(per_owner, dtype=jnp.int32)[None, :]
    slot_ids = (
        ((row_owner * var_count + my_var) * cmp_count + my_core) * per_owner + row_unit
    ).reshape(-1)
    var_ids = owner_map[slot_ids]
    var_rup = var_rupture[var_ids]
    hypo_index = var_source[var_ids, 0]
    slip_index = var_source[var_ids, 1]
    functions = slip_spec.shape[0]
    rup_onehot = (var_rup[:, None] == rupture_iota[None, :]).astype(jnp.int32)
    rup_length = jnp.sum(rup_onehot * lengths[None, :], axis=1)
    hypocenter = hypo_index * rup_length // functions
    same_rup = var_rup[:, None] == rupture_of[None, :]
    ahead_mask = (same_rup & (position[None, :] >= hypocenter[:, None])).astype(jnp.float32)
    behind_mask = (same_rup & (position[None, :] < hypocenter[:, None])).astype(jnp.float32)
    hypo_cos, hypo_sin = cos_sin(
        frequency[None] * (TAU * hypocenter)[:, None, None] % length, length
    )
    slip_rows = slip_spec[slip_index].reshape(slip_index.shape[0], 2, 64, blocks)
    slip_rows = jnp.transpose(slip_rows, (0, 3, 1, 2)).reshape(slip_index.shape[0], blocks, 128)
    first_sum = jnp.einsum("vq,cqkm->vckm", ahead_mask, lagged, precision=highest)
    second_sum = jnp.einsum("vq,cqkm->vckm", behind_mask, leading, precision=highest)
    rows_cos = hypo_cos[:, None]
    rows_sin = hypo_sin[:, None]
    rows_slip = slip_rows[:, None]
    sum_real = first_sum[..., :64] + second_sum[..., :64]
    diff_real = first_sum[..., :64] - second_sum[..., :64]
    sum_imag = first_sum[..., 64:] + second_sum[..., 64:]
    diff_imag = first_sum[..., 64:] - second_sum[..., 64:]
    turned_real = rows_cos * sum_real - rows_sin * diff_imag
    turned_imag = rows_cos * sum_imag + rows_sin * diff_real
    slip_real = rows_slip[..., :64]
    slip_imag = rows_slip[..., 64:]
    totals = lax.psum_scatter(
        jnp.concatenate(
            [
                slip_real * turned_real - slip_imag * turned_imag,
                slip_real * turned_imag + slip_imag * turned_real,
            ],
            axis=-1,
        ),
        "pts",
        scatter_dimension=0,
        tiled=True,
    )
    result = inverse_series(totals.reshape(per_owner * seis_comp, blocks, 128)).reshape(
        per_owner, seis_comp, samples
    )
    return result


def solution(mesh):
    placed = (
        P("cmp", None, ("site", "pts"), None),
        P("cmp", ("site", "pts")),
        P(),
        P("site"),
        P(("site", "pts"), None),
        P("site"),
        P("site", None),
        P("site"),
    )
    return jax.shard_map(
        per_device,
        mesh=mesh,
        in_specs=placed,
        out_specs=P(("site", "pts", "var", "cmp"), None, None),
        check_vma=False,
    )
```

profile of v0, /device:TPU:0, one launch (start us, length us, event | category | flops | bytes accessed | tf_op | source)
XLA Modules:
  0.0 121.4 jit_solution(11977667582550914608)
XLA Ops:
  6.6 0.8 and_select_fusion
  7.4 0.2 convert_reduce_fusion
  7.8 0.7 scatter_custom_fusion.1
  8.5 3.9 %gather_fusion.5 = bf16[16,3,3,4096]{3,0,2,1:T(8,128)(2,1)S(1)} fusion(bf16[3,3,16,4096]{3,2,1,0:T(8,128)(2,1)S(1)} %copy-done, s32[1024]{0:T(1024)S(1)} %pad_clamp_fusion.1), kind=kCustom, calls=%fused_computation.5 | custom fusion | bytes 2359360 | tf_op jit(solution)/shard_map/jit(_take)/gather | solution.py:108
  12.5 0.7 scatter_custom_fusion
  13.1 0.2 select_bitcast_fusion
  13.3 2.2 %copy.52 = bf16[3,3,16,4096]{3,1,0,2:T(4,128)(2,1)} copy(bf16[3,3,16,4096]{3,2,1,0:T(8,128)(2,1)S(1)} %select_bitcast_fusion) | data formatting | bytes 2359296 | tf_op jit(solution)/shard_map/jit(_where)/select_n | solution.py:109
  15.5 6.5 %all-to-all-start = ((bf16[3,3,16,4096]{3,1,0,2:T(4,128)(2,1)}), bf16[3,3,16,4096]{3,1,0,2:T(4,128)(2,1)S(1)}, u32[]{:S(2)}, u32[]{:S(2)}) async-start(bf16[3,3,16,4096]{3,1,0,2:T(4,128)(2,1)} %copy.52), calls=%async_computation | async-start | bytes 3145728 | tf_op jit(solution)/shard_map/all_to_all | solution.py:110
  22.0 0.7 sine_negate_fusion
  22.7 0.5 compare_and_fusion.3
  23.4 30.0 %all-gather = s32[4,1,6]{2,1,0:T(1,128)S(1)} all-gather(s32[1,1,6]{2,1,0:T(1,128)S(1)} %bitcast.102), channel_id=1, replica_groups=mesh['site'=2,'pts'=4,'var'=2,'cmp'=2] {'pts'}, dimensions={0}, use_global_device_ids=true | all-gather | bytes 120 | tf_op jit(solution)/shard_map/all_gather | solution.py:121
  53.4 0.2 reduce-window.4
  53.8 0.6 gather_fusion
  54.5 0.6 gather_fusion.3
  55.2 0.6 gather_fusion.1
  55.8 1.7 %gather_fusion.2 = f32[4,2,4096]{2,1,0:T(2,128)S(1)} fusion(f32[16,2,4096]{2,1,0:T(2,128)} %param.10, s32[1024]{0:T(1024)S(1)} %pad_clamp_fusion.3), kind=kCustom, calls=%fused_computation.2 | custom fusion | bytes 262160 | tf_op jit(solution)/shard_map/gather | solution.py:169
  57.6 0.2 reshape.311
  58.0 0.6 gather_fusion.4
  58.7 0.2 select_reduce_fusion
  58.9 0.2 select_reduce_fusion.2
  59.0 0.8 fusion.56
  59.8 0.9 fusion.61
  60.7 0.9 fusion.54
  61.6 0.5 iota_add_fusion.1
  62.2 1.9 %fusion.48 = (f32[4,64,64]{2,0,1:T(4,128)}, f32[4,64,64]{2,0,1:T(4,128)}) fusion(s32[4]{0:T(128)S(1)} %get-tuple-element.8, s32[64,64]{1,0:T(8,128)S(1)} %iota_add_fusion), kind=kLoop, calls=%fused_computation.89 | loop fusion | flops 229376 | bytes 147472 | tf_op jit(solution)/shard_map/cos | solution.py:16
  64.0 1.1 fusion.41
  65.1 1.8 %copy.53 = bf16[3,3,16,4096]{3,1,2,0:T(4,128)(2,1)} copy(bf16[3,3,16,4096]{3,1,0,2:T(4,128)(2,1)S(1)} %all-to-all-done) | data formatting | bytes 2359296 | tf_op jit(solution)/shard_map/all_to_all | solution.py:110
  67.0 2.6 %gather_fusion.6 = bf16[8,3,3,4096]{3,2,1,0:T(4,128)(2,1)S(1)} fusion(bf16[3,3,16,4096]{3,1,2,0:T(4,128)(2,1)} %copy.53, s32[1024]{0:T(1024)S(1)} %pad_clamp_fusion), kind=kCustom, calls=%fused_computation.6 | custom fusion | bytes 1179680 | tf_op jit(solution)/shard_map/jit(_take)/gather | solution.py:112
  69.6 0.7 fusion
  70.3 0.4 copy.54
  70.7 4.0 %all_to_all.17 = f32[1,3,8,4096]{3,0,1,2:T(1,128)S(1)} all-to-all(f32[1,3,8,4096]{3,0,1,2:T(1,128)S(1)} %copy.54), channel_id=1, replica_groups=mesh['site'=2,'pts'=4,'var'=2,'cmp'=2] {'cmp'}, dimensions={2} | all-to-all | bytes 786432 | tf_op jit(solution)/shard_map/all_to_all | solution.py:114
  74.8 0.3 copy.67
  75.1 0.2 reduce_sum.82
  75.6 0.9 convolution_bitcast_fusion
  76.7 0.9 fusion.1
  77.6 2.4 %all_gather.7 = f32[3,8,64,128]{3,2,0,1:T(8,128)S(1)} all-gather(f32[3,4,64,128]{3,2,0,1:T(8,128)S(1)} %copy.58), channel_id=1, replica_groups=mesh['site'=2,'pts'=4,'var'=2,'cmp'=2] {'cmp'}, dimensions={1}, use_global_device_ids=true | all-gather | bytes 1179648 | tf_op jit(solution)/shard_map/all_gather | solution.py:120
  79.9 0.3 fusion.114
  80.3 1.0 fusion.14
  81.3 0.6 fusion.5
  81.9 0.6 fusion.9
  82.6 0.3 copy-done.4
  82.9 0.5 multiply_subtract_fusion
  83.5 0.3 pad_maximum_fusion
  83.8 0.8 copy.61
  84.7 0.1 fusion.73
  85.0 27.4 %reduce-scatter.2.cloned.1.call-done = f32[1,3,64,128]{3,2,1,0:T(8,128)} async-done(((f32[4,3,64,128]{3,2,1,0:T(8,128)}), f32[1,3,64,128]{3,2,1,0:T(8,128)}) %reduce-scatter.2.cloned.1.call-update) | async-done | bytes 98320 | tf_op jit(solution)/shard_map/reduce_scatter | solution.py:184
  112.4 1.2 fusion.33
  113.6 0.9 fusion.20
  (83 shorter events, 1.8 us)
Async XLA Ops:
  6.5 2.0 %copy-start = (bf16[3,3,16,4096]{3,2,1,0:T(8,128)(2,1)S(1)}, bf16[3,3,16,4096]{3,2,1,0:T(8,128)(2,1)}, u32[]{:S(2)}) copy-start(bf16[3,3,16,4096]{3,2,1,0:T(8,128)(2,1)} %param.8) | copy-start | bytes 3538948
  15.5 7.8 %copy-start.19 = (f32[3,8]{1,0:T(4,128)S(1)}, f32[3,8]{1,0:T(4,128)}, u32[]{:S(2)}) copy-start(f32[3,8]{1,0:T(4,128)} %param.9) | copy-start | bytes 292
  15.5 7.9 %copy-start.20 = (s32[1,6]{1,0:T(1,128)S(1)}, s32[1,6]{1,0:T(1,128)}, u32[]{:S(2)}) copy-start(s32[1,6]{1,0:T(1,128)} %param.12) | copy-start | bytes 76
  15.5 38.3 %copy-start.2 = (s32[16]{0:T(128)S(1)}, s32[16]{0:T(128)}, u32[]{:S(2)}) copy-start(s32[16]{0:T(128)} %param.15) | copy-start | bytes 196
  15.5 39.0 %copy-start.1 = (s32[16,2]{0,1:T(2,128)S(1)}, s32[16,2]{0,1:T(2,128)}, u32[]{:S(2)}) copy-start(s32[16,2]{0,1:T(2,128)} %param.14) | copy-start | bytes 388
  15.5 49.6 %all-to-all-start = ((bf16[3,3,16,4096]{3,1,0,2:T(4,128)(2,1)}), bf16[3,3,16,4096]{3,1,0,2:T(4,128)(2,1)S(1)}, u32[]{:S(2)}, u32[]{:S(2)}) async-start(bf16[3,3,16,4096]{3,1,0,2:T(4,128)(2,1)} %copy.52), calls=%async_computation | async-start | bytes 3145728 | tf_op jit(solution)/shard_map/all_to_all | solution.py:110
  22.0 90.4 %reduce-scatter.2.cloned.1.call-start = ((), (), s32[]{:S(2)}) async-start(), calls=%async_computation.3 | async-start | bytes 491520 | tf_op jit(solution)/shard_map/reduce_scatter | solution.py:184
  53.8 4.9 %copy-start.13 = (s32[8]{0:T(128)}, s32[8]{0:T(128)S(1)}, u32[]{:S(2)}) copy-start(s32[8]{0:T(128)S(1)} %convert_reduce_fusion.1) | copy-start | bytes 100
  55.2 2.9 %copy-start.3 = (s32[16]{0:T(128)S(1)}, s32[16]{0:T(128)}, u32[]{:S(2)}) copy-start(s32[16]{0:T(128)} %param.13) | copy-start | bytes 196
  58.7 5.4 %copy-start.15 = (s32[64]{0:T(128)}, s32[64]{0:T(128)S(1)}, u32[]{:S(2)}) copy-start(s32[64]{0:T(128)S(1)} %iota_multiply_fusion.2) | copy-start | bytes 772
  67.0 2.6 %copy-start.18 = (pred[8]{0:T(512)(128)(4,1)S(1)}, pred[8]{0:T(512)(128)(4,1)}, u32[]{:S(2)}) copy-start(pred[8]{0:T(512)(128)(4,1)} %get-tuple-element.10) | copy-start | bytes 28
  74.8 0.8 copy-start.11
  74.8 0.8 copy-start.12
  75.1 1.4 %copy-start.6 = (f32[64,128]{1,0:T(8,128)S(1)}, f32[64,128]{1,0:T(8,128)}, u32[]{:S(2)}) copy-start(f32[64,128]{1,0:T(8,128)} %get-tuple-element.37) | copy-start | bytes 98308
  75.1 1.4 %copy-start.7 = (f32[64,128]{1,0:T(8,128)S(1)}, f32[64,128]{1,0:T(8,128)}, u32[]{:S(2)}) copy-start(f32[64,128]{1,0:T(8,128)} %get-tuple-element.38) | copy-start | bytes 98308
  75.6 1.1 copy-start.8
  75.6 1.1 copy-start.9
  75.6 1.1 copy-start.10
  80.2 1.0 copy-start.14
  80.2 1.0 copy-start.17
  81.9 0.9 copy-start.4
  81.9 1.0 copy-start.5
  83.5 1.3 %copy-start.16 = (s32[64]{0:T(128)S(1)}, s32[64]{0:T(128)}, u32[]{:S(2)}) copy-start(s32[64]{0:T(128)} %copy-done.15) | copy-start | bytes 772
Sparse Core Ops, SparseCore 0:
  84.7 27.6 reduce-scatter.1
where the time goes:
time: 122 us; the launch traced here: 121 us
  blocking collectives  36.4 us (30%)
  waiting for transfers between devices  27.4 us (22%)
  local copies, waits for them, and re-layouts  19.3 us (16%)
  between operations  13.9 us (11%)
  other arithmetic  12.7 us (10%)
  starting transfers between devices  6.49 us (5%)
  matrix products  5.1 us (4%)
    all_gather x1, blocking collectives, per_device(): counts_all = lax.all_gather(rup_counts, 'pts', axis=0, tiled=True)  30 us
    reduce_scatter x1, waiting for transfers between devices, per_device(): lax.psum_scatter(jnp.concatenate([slip_real * turned_real - slip_imag * t...  27.4 us
    all_to_all x1, starting transfers between devices, per_device(): lax.all_to_all(outgoing, 'pts', split_axis=2, concat_axis=2, tiled=True)  6.49 us
    all_to_all x1, blocking collectives, per_device(): lax.all_to_all(partial_value[None], 'cmp', split_axis=2, concat_axis=0, t...  4.05 us
    gather x1, local copies, waits for them, and re-layouts, per_device(): outgoing = jnp.take(sgt, send_rows, axis=2)  3.92 us
    cos x3, other arithmetic, cos_sin(): return (jnp.cos(angles), jnp.sin(angles))  3.1 us
    gather x1, local copies, waits for them, and re-layouts, per_device(): picked = jnp.take(received, pick_rows, axis=2)  2.62 us
  transfers between devices with their start and end apart: 2, of which 1 were waited for; matrix products, arithmetic and copies ran while one was open for 11% of the time, Pallas kernels for 0%

commit v1 on v0

v1 whole, which is shorter than its diff:
```python
import math

import jax
import jax.numpy as jnp
import numpy as np
from jax import lax
from jax.experimental import pallas as pl
from jax.experimental.pallas import tpu as pltpu
from jax.sharding import PartitionSpec as P

TAU = 4
MOSTP = 2
LANES = 128

highest = lax.Precision.HIGHEST


def unit_tables(numerator, period):
    angles = (numerator % period).astype(np.float64) * (2.0 * math.pi / period)
    return np.cos(angles), np.sin(angles)


def transform_tables(comps, rows_in, samples):
    length = 2 * samples
    blocks = length // LANES
    rows_out = blocks // 2
    outer = np.arange(blocks)
    lane = np.arange(LANES)
    half = np.concatenate([np.arange(0, 64, 2), np.arange(1, 64, 2)])
    c1, s1 = unit_tables(outer[:, None] * np.arange(rows_in)[None, :], blocks)
    first = np.concatenate([c1, -s1], axis=0)
    first = np.kron(np.eye(comps), first)
    tc, ts = unit_tables(outer[:, None] * lane[None, :], length)
    c2, s2 = unit_tables(lane[:, None] * half[None, :], 128)
    real_cols = np.concatenate([c2, s2], axis=0)
    imag_cols = np.concatenate([-s2, c2], axis=0)
    second = np.concatenate([real_cols, imag_cols, -imag_cols, real_cols], axis=1)
    c3, s3 = c2.T, s2.T
    third = np.concatenate(
        [np.concatenate([c3, s3], axis=1), np.concatenate([-s3, c3], axis=1)], axis=0
    )
    c4, s4 = unit_tables(np.arange(rows_out)[:, None] * outer[None, :], blocks)
    last = np.concatenate([c4, -s4], axis=1)
    weights = np.full((blocks, 2 * half.size), 2.0 / length)
    weights[0, 0] = weights[0, half.size] = 1.0 / length
    return [np.asarray(x, np.float32) for x in (first, tc, ts, second, third, last, weights)]


def split_two(x):
    high = x.astype(jnp.bfloat16)
    low = (x - high.astype(jnp.float32)).astype(jnp.bfloat16)
    return high, low


def partial_kernel(
    slots, delays, ruptures, functions, var_count, cmp_count,
    table_s, rup_s, src_s, map_s, table_ref, slab_ref, sgt_ref, out_ref, lhs_ref,
):
    comp_half, slab_dev, samples = sgt_ref.shape
    group = out_ref.shape[0]
    rows = out_ref.shape[1] // pl.num_programs(1)
    points = slab_ref.shape[1]
    width = points // slots
    block = pl.program_id(0)
    comp = pl.program_id(1)

    @pl.when(comp == 0)
    def _():
        my_owner = lax.axis_index("pts")
        my_var = lax.axis_index("var")
        point = lax.broadcasted_iota(jnp.int32, (1, points), 1)
        rup_of = jnp.zeros((1, points), jnp.int32)
        pos = jnp.zeros((1, points), jnp.int32)
        lens = [jnp.int32(0)] * ruptures
        for o in range(slots):
            start = jnp.int32(o * width)
            for r in range(ruptures):
                count = table_s[comp_half, o * width + r].astype(jnp.int32)
                stop = start + count
                inside = (point >= start) & (point < stop)
                rup_of = jnp.where(inside, r, rup_of)
                pos = jnp.where(inside, point - start + lens[r], pos)
                lens[r] = lens[r] + count
                start = stop
        index = lax.broadcasted_iota(jnp.int32, (delays * group, 1), 0)
        member = index % group
        delay = index // group
        rup_col = jnp.zeros_like(index)
        hyp_col = jnp.zeros_like(index)
        for v in range(group):
            slot = block * group + v
            slot = ((slot // cmp_count) * var_count + my_var) * cmp_count + slot % cmp_count
            var_id = map_s[slot]
            rup = rup_s[var_id]
            length = lens[0]
            for r in range(1, ruptures):
                length = jnp.where(rup == r, lens[r], length)
            hyp = lax.div(src_s[2 * var_id] * length, jnp.int32(functions))
            rup_col = jnp.where(member == v, rup, rup_col)
            hyp_col = jnp.where(member == v, hyp, hyp_col)
        chosen = (rup_of == rup_col) & (jnp.abs(pos - hyp_col) == delay)
        chosen = chosen.astype(jnp.float32)
        row = lax.broadcasted_iota(jnp.int32, (slab_dev, 1), 0) + my_owner * slab_dev
        named = slab_ref[...] == row
        moments = jnp.concatenate(
            [jnp.where(named, table_ref[j:j + 1, :], 0.0) for j in range(comp_half)], axis=0
        )
        weights = lax.dot_general(
            chosen, moments, (((1,), (1,)), ((), ())),
            precision=highest, preferred_element_type=jnp.float32,
        )
        high, low = split_two(weights)
        inner = weights.shape[1]
        lhs_ref[:, :inner] = high
        lhs_ref[:, inner:] = low

    series = sgt_ref[...].reshape(comp_half * slab_dev, samples)
    series = jnp.concatenate([series, series], axis=0)
    product = jnp.dot(lhs_ref[...], series, preferred_element_type=jnp.float32)
    tail = jnp.zeros((group, rows * LANES - samples), jnp.float32)
    total = None
    for d in range(delays):
        piece = jnp.concatenate([product[d * group:(d + 1) * group], tail], axis=1)
        if d:
            piece = pltpu.roll(piece, TAU * d, 1)
        total = piece if total is None else total + piece
    for c in range(pl.num_programs(1)):
        @pl.when(comp == c)
        def _():
            for a in range(rows):
                out_ref[:, c * rows + a, :] = total[:, a * LANES:(a + 1) * LANES]


def finish_kernel(
    comps, var_count, cmp_count,
    src_s, map_s, parts_ref, first_ref, tc_ref, ts_ref, second_ref, third_ref, last_ref,
    weight_ref, slip_hbm, out_ref, slip_ref, sem,
):
    blocks = tc_ref.shape[0]
    rows_out = blocks // 2
    slot = lax.axis_index("pts") * var_count + lax.axis_index("var")
    slot = slot * cmp_count + lax.axis_index("cmp")
    function = src_s[2 * map_s[slot] + 1]
    copy = pltpu.make_async_copy(slip_hbm.at[function], slip_ref, sem)
    copy.start()
    signal = parts_ref[0]
    for p in range(1, parts_ref.shape[0]):
        signal = signal + parts_ref[p]
    dot = lambda a, b: jnp.dot(a, b, precision=highest, preferred_element_type=jnp.float32)
    first = dot(first_ref[...], signal)
    tc = tc_ref[...]
    ts = ts_ref[...]
    joined = []
    for c in range(comps):
        re = first[2 * c * blocks:(2 * c + 1) * blocks]
        im = first[(2 * c + 1) * blocks:(2 * c + 2) * blocks]
        joined.append(jnp.concatenate([re * tc + im * ts, im * tc - re * ts], axis=1))
    spectra = dot(jnp.concatenate(joined, axis=0), second_ref[...])
    copy.wait()
    slips = []
    for part in range(2):
        wide = jnp.concatenate(
            [slip_ref[part:part + 1, a * LANES:(a + 1) * LANES] for a in range(rows_out)], axis=0
        )
        turned = wide.T
        turned = jnp.concatenate([turned[:blocks], turned[blocks:]], axis=1)
        slips.append(jnp.concatenate([turned, turned], axis=1) * weight_ref[...])
    slips = [jnp.concatenate([s] * comps, axis=0) for s in slips]
    scaled = spectra[:, :LANES] * slips[0] + spectra[:, LANES:] * slips[1]
    middle = dot(scaled, third_ref[...])
    for c in range(comps):
        re = middle[c * blocks:(c + 1) * blocks, :LANES]
        im = middle[c * blocks:(c + 1) * blocks, LANES:]
        back = jnp.concatenate([re * tc - im * ts, re * ts + im * tc], axis=0)
        out_ref[c] = dot(last_ref[...], back)


def per_device(sgt, moment, slip_spec, rp_slab, rup_counts, var_rupture, var_source, owner_map):
    comp_half, comps, slab_dev, samples = sgt.shape
    rp_dev = moment.shape[1]
    owners = lax.axis_size("pts")
    var_count = lax.axis_size("var")
    cmp_count = lax.axis_size("cmp")
    ruptures = rup_counts.shape[1]
    functions = slip_spec.shape[0]
    targets = owners * cmp_count
    assert owner_map.shape[0] == targets * var_count and rp_dev >= ruptures
    delays = MOSTP * owners
    rows = -(-(samples + TAU * (delays - 1)) // LANES)
    group = 8 if targets % 8 == 0 else targets
    counts = jnp.pad(rup_counts.astype(jnp.float32), ((0, 0), (0, rp_dev - ruptures)))
    table = lax.all_gather(
        jnp.concatenate([moment, counts], axis=0), "pts", axis=1, tiled=True
    )
    points = rp_slab.shape[0]
    sources = var_source.reshape(-1)
    smem = pl.BlockSpec(memory_space=pltpu.SMEM)
    whole = lambda shape: pl.BlockSpec(shape, lambda *_: (0,) * len(shape))

    partial = pl.pallas_call(
        lambda *refs: partial_kernel(
            owners, delays, ruptures, functions, var_count, cmp_count, *refs
        ),
        grid=(targets // group, comps),
        in_specs=[
            smem, smem, smem, smem,
            whole(table.shape),
            whole((1, points)),
            pl.BlockSpec((comp_half, pl.squeezed, slab_dev, samples), lambda b, c: (0, c, 0, 0)),
        ],
        out_specs=pl.BlockSpec((group, comps * rows, LANES), lambda b, c: (b, 0, 0)),
        out_shape=jax.ShapeDtypeStruct((targets, comps * rows, LANES), jnp.float32),
        scratch_shapes=[pltpu.VMEM((delays * group, 2 * comp_half * slab_dev), jnp.bfloat16)],
    )
    parts = partial(
        table, var_rupture, sources, owner_map, table, rp_slab.reshape(1, points), sgt
    )
    parts = lax.all_to_all(parts, ("pts", "cmp"), split_axis=0, concat_axis=0, tiled=True)
    tables = transform_tables(comps, rows, samples)
    result = pl.pallas_call(
        lambda *refs: finish_kernel(comps, var_count, cmp_count, *refs),
        in_specs=[smem, smem]
        + [pl.BlockSpec(memory_space=pltpu.VMEM)] * (1 + len(tables))
        + [pl.BlockSpec(memory_space=pl.ANY)],
        out_specs=pl.BlockSpec(memory_space=pltpu.VMEM),
        out_shape=jax.ShapeDtypeStruct((comps, samples // LANES, LANES), jnp.float32),
        scratch_shapes=[pltpu.VMEM(slip_spec.shape[1:], jnp.float32), pltpu.SemaphoreType.DMA(())],
    )(sources, owner_map, parts, *tables, slip_spec)
    return result.reshape(1, comps, samples)


def solution(mesh):
    placed = (
        P("cmp", None, ("site", "pts"), None),
        P("cmp", ("site", "pts")),
        P(),
        P("site"),
        P(("site", "pts"), None),
        P("site"),
        P("site", None),
        P("site"),
    )
    return jax.shard_map(
        per_device,
        mesh=mesh,
        in_specs=placed,
        out_specs=P(("site", "pts", "var", "cmp"), None, None),
        check_vma=False,
    )
```

time: 122 us -> 42.8 us (0.35)
  waiting for transfers between devices: 27.4 us -> 0 us
  local copies, waits for them, and re-layouts: 19.3 us -> 2.05 us
  between operations: 13.9 us -> 0.01 us
  other arithmetic: 12.7 us -> 1.35 us
  Pallas kernels: 0 us -> 8.11 us
  starting transfers between devices: 6.49 us -> 0 us
  blocking collectives: 36.4 us -> 30.9 us
  matrix products: 5.1 us -> 0 us
    reduce_scatter x1 -> x0, waiting for transfers between devices: 27.4 us -> none  [per_device(): lax.psum_scatter(jnp.concatenate([slip_real * turned_real - slip_imag * t...]
    all_gather x2 -> x1, blocking collectives: 32.4 us -> 13.6 us  [per_device(): lax.all_gather(jnp.concatenate([moment, counts], axis=0), 'pts', axis=1,...]
    all_to_all x1, blocking collectives: 4.05 us -> 17.3 us  [per_device(): lax.all_to_all(parts, ('pts', 'cmp'), split_axis=0, concat_axis=0, tiled=...]
    gather x7 -> x0, local copies, waits for them, and re-layouts: 10.8 us -> none  [the longest x1 3.92 us: per_device(): outgoing = jnp.take(sgt, send_rows, axis=2)]
    pallas_call x0 -> x2, Pallas kernels: none -> 8.11 us  [the longest x1 4.32 us: per_device(): partial(table, var_rupture, sources, owner_map, table, rp_slab.reshape(1,...]
    all_to_all x1 -> x0, starting transfers between devices: 6.49 us -> none  [per_device(): lax.all_to_all(outgoing, 'pts', split_axis=2, concat_axis=2, tiled=True)]
    dot_general x6 -> x0, matrix products: 5.1 us -> none  [the longest x1 1.2 us: inverse_series(): middle = jnp.einsum('skm,mb->skb', scaled, third_table, precision=highest)]
    cos x3 -> x0, other arithmetic: 3.1 us -> none  [cos_sin(): return (jnp.cos(angles), jnp.sin(angles))]
  transfers between devices with their start and end apart: 2 -> 0, of which waited for: 1 -> 0; matrix products, arithmetic and copies ran while one was open for 11% -> 0% of each run, Pallas kernels for 0% -> 0%
where the time goes in v1:
time: 42.8 us; the launch traced here: 42.4 us
  blocking collectives  30.9 us (72%)
  Pallas kernels  8.11 us (19%)
  local copies, waits for them, and re-layouts  2.05 us (5%)
  other arithmetic  1.35 us (3%)
    all_to_all x1, blocking collectives, per_device(): lax.all_to_all(parts, ('pts', 'cmp'), split_axis=0, concat_axis=0, tiled=...  17.3 us
    all_gather x1, blocking collectives, per_device(): lax.all_gather(jnp.concatenate([moment, counts], axis=0), 'pts', axis=1,...  13.6 us
    pallas_call x1, Pallas kernels, per_device(): partial(table, var_rupture, sources, owner_map, table, rp_slab.reshape(1,...  4.32 us
    pallas_call x1, Pallas kernels, per_device(): pl.pallas_call(lambda *refs: finish_kernel(comps, var_count, cmp_count, *...  3.79 us
    unnamed x2, local copies, waits for them, and re-layouts  1.42 us

profile of v1, /device:TPU:0, one launch (start us, length us, event | category | flops | bytes accessed | tf_op | source)
XLA Modules:
  0.0 42.4 jit_solution(2114185461580759144)
XLA Ops:
  0.0 0.7 %convert_element_type.5 = f32[1,6]{1,0:T(1,128)S(1)} convert(s32[1,6]{1,0:T(1,128)} %param.19) | non-fusion elementwise | flops 6 | bytes 48 | tf_op jit(solution)/shard_map/convert_element_type | solution.py:191
  0.7 0.7 %fusion = f32[1,8,4]{1,2,0:T(4,128)S(1)} fusion(f32[1,6]{1,0:T(1,128)S(1)} %convert_element_type.5, f32[3,8]{1,0:T(4,128)} %param.16), kind=kLoop, calls=%fused_computation.1 | loop fusion | flops 96 | bytes 248
  1.3 13.6 %all-gather = f32[4,8,4]{1,2,0:T(4,128)S(1)} all-gather(f32[1,8,4]{1,2,0:T(4,128)S(1)} %fusion), channel_id=1, replica_groups=mesh['site'=2,'pts'=4,'var'=2,'cmp'=2] {'pts'}, dimensions={0}, use_global_device_ids=true | all-gather | bytes 640 | tf_op jit(solution)/shard_map/all_gather | solution.py:192
  15.0 0.7 %reshape.13 = f32[32,4]{0,1:T(4,128)} reshape(f32[4,8,4]{1,0,2:T(4,128)S(1)} %copy.23) | data formatting | bytes 1024
  15.6 0.8 %copy.22 = s32[16,2]{1,0:T(8,128)S(1)} copy(s32[16,2]{0,1:T(2,128)} %param.21) | data formatting | bytes 256 | tf_op args[6]
  16.4 0.6 %reshape.9.refs_2_.refs_0_ = s32[32]{0:T(128)} reshape(s32[16,2]{1,0:T(8,128)S(1)} %copy.22) | data formatting | bytes 256 | tf_op jit(solution)/shard_map/reshape | solution.py:196
  17.0 4.3 %shard_map.145 = f32[8,99,128]{2,1,0:T(8,128)} custom-call(f32[4,32]{1,0:T(4,128)} %bitcast.9, s32[16]{0:T(128)} %refs_1_.2, s32[32]{0:T(128)} %reshape.9.refs_2_.refs_0_, s32[16]{0:T(128)} %refs_1_.3, f32[4,32]{1,0:T(4,128)} %bitcast.10, s32[1,32]{1,0:T(1,128)} %bitcast.11, bf16[3,3,16,4096]{3,2,1,0:T(8,128)(2,1)} %refs_6_.2), custom_call_target="tpu_custom_call" | custom-call | tf_op jit(solution)/shard_map/pallas_call | solution.py:215
  21.3 17.3 %all_to_all.5.refs_2_ = f32[8,99,128]{2,1,0:T(8,128)} all-to-all(f32[8,99,128]{2,1,0:T(8,128)} %shard_map.145), channel_id=1, replica_groups=mesh['site'=2,'pts'=4,'var'=2,'cmp'=2] {'pts','cmp'}, dimensions={0} | all-to-all | bytes 811008 | tf_op jit(solution)/shard_map/all_to_all | solution.py:218
  38.7 3.8 %shard_map.146 = f32[3,32,128]{2,1,0:T(8,128)} custom-call(s32[32]{0:T(128)} %reshape.9.refs_2_.refs_0_, s32[16]{0:T(128)} %refs_1_.3, f32[8,99,128]{2,1,0:T(8,128)} %all_to_all.5.refs_2_, f32[384,99]{1,0:T(8,128)} %constant.17.clone.refs_3_, f32[64,128]{1,0:T(8,128)} %constant.18.clone.refs_4_, f32[64,128]{1,0:T(8,128)} %constant.19.clone.refs_5_, ...), custom_call_target="tpu_custom_call" | custom-call | tf_op jit(solution)/shard_map/pallas_call | solution.py:220
  (1 shorter events, 0.0 us)

commit v2 on v1

v2 whole, which is shorter than its diff:
```python
import math

import jax
import jax.numpy as jnp
import numpy as np
from jax import lax
from jax.experimental import pallas as pl
from jax.experimental.pallas import tpu as pltpu
from jax.sharding import PartitionSpec as P

TAU = 4
MOSTP = 2
LANES = 128

highest = lax.Precision.HIGHEST


def unit_tables(numerator, period):
    angles = (numerator % period).astype(np.float64) * (2.0 * math.pi / period)
    return np.cos(angles), np.sin(angles)


def transform_tables(comps, rows_in, samples):
    length = 2 * samples
    blocks = length // LANES
    rows_out = blocks // 2
    outer = np.arange(blocks)
    lane = np.arange(LANES)
    half = np.concatenate([np.arange(0, 64, 2), np.arange(1, 64, 2)])
    c1, s1 = unit_tables(outer[:, None] * np.arange(rows_in)[None, :], blocks)
    first = np.concatenate([c1, -s1], axis=0)
    first = np.kron(np.eye(comps), first)
    tc, ts = unit_tables(outer[:, None] * lane[None, :], length)
    c2, s2 = unit_tables(lane[:, None] * half[None, :], 128)
    real_cols = np.concatenate([c2, s2], axis=0)
    imag_cols = np.concatenate([-s2, c2], axis=0)
    second = np.concatenate([real_cols, imag_cols, -imag_cols, real_cols], axis=1)
    c3, s3 = c2.T, s2.T
    third = np.concatenate(
        [np.concatenate([c3, s3], axis=1), np.concatenate([-s3, c3], axis=1)], axis=0
    )
    c4, s4 = unit_tables(np.arange(rows_out)[:, None] * outer[None, :], blocks)
    last = np.concatenate([c4, -s4], axis=1)
    turns = [np.asarray(x, np.float32) for x in (tc, ts)]
    return turns + [table_pair(x) for x in (first, second, third, last)]


def table_pair(x):
    high = x.astype(jnp.bfloat16)
    low = (x - high.astype(np.float64)).astype(jnp.bfloat16)
    return np.stack([high, low])


def reversed_bits(value, count):
    bits = count.bit_length() - 1
    total = 0
    for b in range(bits):
        total = total + (((value >> b) & 1) << (bits - 1 - b))
    return total


def split_two(x):
    high = x.astype(jnp.bfloat16)
    low = (x - high.astype(jnp.float32)).astype(jnp.bfloat16)
    return high, low


def partial_kernel(
    slots, delays, ruptures, functions, var_count, cmp_count, single,
    table_s, slab_s, rup_s, src_s, map_s, table_ref, sgt_ref, out_ref, lhs_ref,
):
    comp_half, slab_dev, samples = sgt_ref.shape
    group = out_ref.shape[0]
    rows = out_ref.shape[1] // pl.num_programs(1)
    points = slab_s.shape[0]
    width = points // slots
    block = 0 if single else pl.program_id(0)
    comp = pl.program_id(1)

    @pl.when(comp == 0)
    def _():
        my_owner = lax.axis_index("pts")
        my_var = lax.axis_index("var")
        my_core = lax.axis_index("cmp")
        point = lax.broadcasted_iota(jnp.int32, (1, points), 1)
        rup_of = jnp.zeros((1, points), jnp.int32)
        pos = jnp.zeros((1, points), jnp.int32)
        slab = jnp.zeros((1, points), jnp.int32)
        lens = [jnp.int32(0)] * ruptures
        for o in range(slots):
            base = jnp.bitwise_xor(my_owner, o) * width
            start = base
            for l in range(width):
                slab = jnp.where(point == base + l, slab_s[o * width + l], slab)
            for r in range(ruptures):
                count = table_s[comp_half, base + r].astype(jnp.int32)
                stop = start + count
                inside = (point >= start) & (point < stop)
                rup_of = jnp.where(inside, r, rup_of)
                pos = jnp.where(inside, point - start + lens[r], pos)
                lens[r] = lens[r] + count
                start = stop
        index = lax.broadcasted_iota(jnp.int32, (delays * group, 1), 0)
        member = index % group
        delay = index // group
        rup_col = jnp.zeros_like(index)
        hyp_col = jnp.zeros_like(index)
        for v in range(group):
            piece = block * group + v
            owner = jnp.bitwise_xor(my_owner, reversed_bits(piece % slots, slots))
            slot = (owner * var_count + my_var) * cmp_count
            slot = slot + jnp.bitwise_xor(my_core, piece // slots)
            var_id = map_s[slot]
            rup = rup_s[var_id]
            length = lens[0]
            for r in range(1, ruptures):
                length = jnp.where(rup == r, lens[r], length)
            hyp = lax.div(src_s[0, var_id] * length, jnp.int32(functions))
            rup_col = jnp.where(member == v, rup, rup_col)
            hyp_col = jnp.where(member == v, hyp, hyp_col)
        chosen = (rup_of == rup_col) & (jnp.abs(pos - hyp_col) == delay)
        chosen = chosen.astype(jnp.float32)
        row = lax.broadcasted_iota(jnp.int32, (slab_dev, 1), 0) + my_owner * slab_dev
        named = slab == row
        moments = jnp.concatenate(
            [jnp.where(named, table_ref[j:j + 1, :], 0.0) for j in range(comp_half)], axis=0
        )
        weights = lax.dot_general(
            chosen, moments, (((1,), (1,)), ((), ())),
            precision=highest, preferred_element_type=jnp.float32,
        )
        high, low = split_two(weights)
        inner = weights.shape[1]
        lhs_ref[:, :inner] = high
        lhs_ref[:, inner:] = low

    series = sgt_ref[...].reshape(comp_half * slab_dev, samples)
    series = jnp.concatenate([series, series], axis=0)
    product = jnp.dot(lhs_ref[...], series, preferred_element_type=jnp.float32)
    tail = jnp.zeros((group, rows * LANES - samples), jnp.float32)
    total = None
    for d in range(delays):
        piece = jnp.concatenate([product[d * group:(d + 1) * group], tail], axis=1)
        if d:
            piece = pltpu.roll(piece, TAU * d, 1)
        total = piece if total is None else total + piece
    for c in range(pl.num_programs(1)):
        @pl.when(comp == c)
        def _():
            for a in range(rows):
                out_ref[:, c * rows + a, :] = total[:, a * LANES:(a + 1) * LANES]


def slip_kernel(var_count, cmp_count, src_s, map_s, slip_hbm, out_ref, slip_ref, sem):
    blocks = out_ref.shape[1]
    rows_out = blocks // 2
    length = LANES * blocks
    slot = lax.axis_index("pts") * var_count + lax.axis_index("var")
    slot = slot * cmp_count + lax.axis_index("cmp")
    function = src_s[1, map_s[slot]]
    copy = pltpu.make_async_copy(slip_hbm.at[function], slip_ref, sem)
    copy.start()
    row = lax.broadcasted_iota(jnp.int32, (blocks, LANES), 0)
    lane = lax.broadcasted_iota(jnp.int32, (blocks, LANES), 1)
    steady = (row == 0) & (lane % (LANES // 2) == 0)
    weight = jnp.where(steady, 1.0 / length, 2.0 / length)
    copy.wait()
    for part in range(2):
        wide = jnp.concatenate(
            [slip_ref[part:part + 1, a * LANES:(a + 1) * LANES] for a in range(rows_out)], axis=0
        )
        turned = wide.T
        turned = jnp.concatenate([turned[:blocks], turned[blocks:]], axis=1)
        out_ref[part] = jnp.concatenate([turned, turned], axis=1) * weight


def dot_pairs(a, b):
    dot = lambda x, y: jnp.dot(x, y, preferred_element_type=jnp.float32)
    return dot(a[0], b[0]) + (dot(a[0], b[1]) + dot(a[1], b[0]))


def finish_kernel(
    comps, kept_ref, came_ref, slip_ref, tc_ref, ts_ref, first_ref, second_ref, third_ref,
    last_ref, out_ref,
):
    blocks = tc_ref.shape[0]
    signal = kept_ref[0] + came_ref[0]
    first = dot_pairs(first_ref, split_two(signal))
    tc = tc_ref[...]
    ts = ts_ref[...]
    joined = []
    for c in range(comps):
        re = first[2 * c * blocks:(2 * c + 1) * blocks]
        im = first[(2 * c + 1) * blocks:(2 * c + 2) * blocks]
        joined.append(jnp.concatenate([re * tc + im * ts, im * tc - re * ts], axis=1))
    spectra = dot_pairs(split_two(jnp.concatenate(joined, axis=0)), second_ref)
    slips = [jnp.concatenate([slip_ref[part]] * comps, axis=0) for part in range(2)]
    scaled = spectra[:, :LANES] * slips[0] + spectra[:, LANES:] * slips[1]
    middle = dot_pairs(split_two(scaled), third_ref)
    for c in range(comps):
        re = middle[c * blocks:(c + 1) * blocks, :LANES]
        im = middle[c * blocks:(c + 1) * blocks, LANES:]
        back = jnp.concatenate([re * tc - im * ts, re * ts + im * tc], axis=0)
        out_ref[c] = dot_pairs(last_ref, split_two(back))


def per_device(sgt, moment, slip_spec, rp_slab, rup_counts, var_rupture, var_source, owner_map):
    comp_half, comps, slab_dev, samples = sgt.shape
    rp_dev = moment.shape[1]
    owners = lax.axis_size("pts")
    var_count = lax.axis_size("var")
    cmp_count = lax.axis_size("cmp")
    ruptures = rup_counts.shape[1]
    functions = slip_spec.shape[0]
    targets = owners * cmp_count
    assert owner_map.shape[0] == targets * var_count and rp_dev >= ruptures
    assert cmp_count == 2 and owners & (owners - 1) == 0
    delays = MOSTP * owners
    rows = -(-(samples + TAU * (delays - 1)) // LANES)
    group = 8 if targets % 8 == 0 else targets
    counts = jnp.pad(
        rup_counts.astype(jnp.float32), ((comp_half, 0), (0, rp_dev - ruptures))
    )
    table = jnp.pad(moment, ((0, 1), (0, 0))) + counts
    bits = [1 << b for b in range(owners.bit_length() - 1)]
    swap = lambda x, axis, size, bit: lax.ppermute(x, axis, [(i, i ^ bit) for i in range(size)])
    for bit in bits:
        table = jnp.concatenate([table, swap(table, "pts", owners, bit)], axis=1)
    sources = var_source.T
    smem = pl.BlockSpec(memory_space=pltpu.SMEM)
    vmem = pl.BlockSpec(memory_space=pltpu.VMEM)

    slips = pl.pallas_call(
        lambda *refs: slip_kernel(var_count, cmp_count, *refs),
        in_specs=[smem, smem, pl.BlockSpec(memory_space=pl.ANY)],
        out_specs=vmem,
        out_shape=jax.ShapeDtypeStruct((2, 2 * samples // LANES, LANES), jnp.float32),
        scratch_shapes=[pltpu.VMEM(slip_spec.shape[1:], jnp.float32), pltpu.SemaphoreType.DMA(())],
    )(sources, owner_map, slip_spec)

    partial = pl.pallas_call(
        lambda *refs: partial_kernel(
            owners, delays, ruptures, functions, var_count, cmp_count, targets == group, *refs
        ),
        grid=(targets // group, comps),
        in_specs=[
            smem, smem, smem, smem, smem,
            pl.BlockSpec(table.shape, lambda b, c: (0, 0)),
            pl.BlockSpec((comp_half, pl.squeezed, slab_dev, samples), lambda b, c: (0, c, 0, 0)),
        ],
        out_specs=pl.BlockSpec((group, comps * rows, LANES), lambda b, c: (b, 0, 0)),
        out_shape=jax.ShapeDtypeStruct((targets, comps * rows, LANES), jnp.float32),
        scratch_shapes=[pltpu.VMEM((delays * group, 2 * comp_half * slab_dev), jnp.bfloat16)],
    )
    kept = partial(table, rp_slab, var_rupture, sources, owner_map, table, sgt)
    came = None
    for axis, size, bit in [("cmp", cmp_count, 1)] + [("pts", owners, bit) for bit in bits]:
        if came is not None:
            kept = kept + came
        middle = kept.shape[0] // 2
        came = swap(kept[middle:], axis, size, bit)
        kept = kept[:middle]
    tables = transform_tables(comps, rows, samples)
    result = pl.pallas_call(
        lambda *refs: finish_kernel(comps, *refs),
        in_specs=[vmem] * (3 + len(tables)),
        out_specs=vmem,
        out_shape=jax.ShapeDtypeStruct((comps, samples // LANES, LANES), jnp.float32),
    )(kept, came, slips, *tables)
    return result.reshape(1, comps, samples)


def solution(mesh):
    placed = (
        P("cmp", None, ("site", "pts"), None),
        P("cmp", ("site", "pts")),
        P(),
        P("site"),
        P(("site", "pts"), None),
        P("site"),
        P("site", None),
        P("site"),
    )
    return jax.shard_map(
        per_device,
        mesh=mesh,
        in_specs=placed,
        out_specs=P(("site", "pts", "var", "cmp"), None, None),
        check_vma=False,
    )
```

time: 42.8 us -> 33.9 us (0.79)
  blocking collectives: 30.9 us -> 0 us
  starting transfers between devices: 0 us -> 10.9 us
  waiting for transfers between devices: 0 us -> 7.85 us
  other arithmetic: 1.35 us -> 3.05 us
  Pallas kernels: 8.11 us -> 9.51 us
    all_to_all x1 -> x0, blocking collectives: 17.3 us -> none  [per_device(): lax.all_to_all(parts, ('pts', 'cmp'), split_axis=0, concat_axis=0, tiled=...]
    all_gather x1 -> x0, blocking collectives: 13.6 us -> none  [per_device(): lax.all_gather(jnp.concatenate([moment, counts], axis=0), 'pts', axis=1,...]
    ppermute x0 -> x5, starting transfers between devices: none -> 10.9 us  [per_device(): lax.ppermute(x, axis, [(i, i ^ bit) for i in range(size)])]
    ppermute x0 -> x5, waiting for transfers between devices: none -> 7.85 us  [per_device(): lax.ppermute(x, axis, [(i, i ^ bit) for i in range(size)])]
    add x0 -> x3, other arithmetic: none -> 1.67 us  [the longest x2 0.98 us: per_device(): kept = kept + came]
    slice x0 -> x3, local copies, waits for them, and re-layouts: none -> 1.58 us  [per_device(): came = swap(kept[middle:], axis, size, bit)]
    pallas_call x2 -> x3, Pallas kernels: 8.11 us -> 9.51 us  [the longest x1 4.34 us: per_device(): kept = partial(table, rp_slab, var_rupture, sources, owner_map, table, sgt)]
    unnamed x2, local copies, waits for them, and re-layouts: 1.42 us -> 0.6 us
  transfers between devices with their start and end apart: 0 -> 5, of which waited for: 0 -> 4; matrix products, arithmetic and copies ran while one was open for 0% -> 0% of each run, Pallas kernels for 0% -> 7%
where the time goes in v2:
time: 33.9 us; the launch traced here: 33.5 us
  starting transfers between devices  10.9 us (32%)
  Pallas kernels  9.51 us (28%)
  waiting for transfers between devices  7.85 us (23%)
  other arithmetic  3.05 us (9%)
  local copies, waits for them, and re-layouts  2.18 us (6%)
    ppermute x5, starting transfers between devices, per_device(): lax.ppermute(x, axis, [(i, i ^ bit) for i in range(size)])  10.9 us
    ppermute x5, waiting for transfers between devices, per_device(): lax.ppermute(x, axis, [(i, i ^ bit) for i in range(size)])  7.85 us
    pallas_call x1, Pallas kernels, per_device(): kept = partial(table, rp_slab, var_rupture, sources, owner_map, table, sgt)  4.34 us
    pallas_call x1, Pallas kernels, per_device(): pl.pallas_call(lambda *refs: finish_kernel(comps, *refs), in_specs=[vmem]...  2.82 us
    pallas_call x1, Pallas kernels, per_device(): pl.pallas_call(lambda *refs: slip_kernel(var_count, cmp_count, *refs), in...  2.35 us
    slice x3, local copies, waits for them, and re-layouts, per_device(): came = swap(kept[middle:], axis, size, bit)  1.58 us
    add x2, other arithmetic, per_device(): kept = kept + came  0.98 us
    concatenate x2, other arithmetic, per_device(): table = jnp.concatenate([table, swap(table, 'pts', owners, bit)], axis=1)  0.73 us
  transfers between devices with their start and end apart: 5, of which 4 were waited for; matrix products, arithmetic and copies ran while one was open for 0% of the time, Pallas kernels for 7%

profile of v2, /device:TPU:0, one launch (start us, length us, event | category | flops | bytes accessed | tf_op | source)
XLA Modules:
  0.0 33.5 jit_solution(1131571500460632248)
XLA Ops:
  0.0 0.7 %convert_element_type.7 = f32[1,6]{1,0:T(1,128)S(1)} convert(s32[1,6]{1,0:T(1,128)} %param.18) | non-fusion elementwise | flops 6 | bytes 48 | tf_op jit(solution)/shard_map/convert_element_type | solution.py:222
  0.7 0.7 %pad_add_fusion = f32[4,8]{1,0:T(4,128)S(1)} fusion(f32[1,6]{1,0:T(1,128)S(1)} %convert_element_type.7, f32[3,8]{1,0:T(4,128)} %param.15), kind=kLoop, calls=%fused_computation.4 | loop fusion | flops 32 | bytes 248 | tf_op jit(solution)/shard_map/add | solution.py:224
  1.3 3.1 %collective-permute-start = (f32[4,8]{1,0:T(4,128)S(1)}, f32[4,8]{1,0:T(4,128)S(1)}, u32[]{:S(2)}, u32[]{:S(2)}) collective-permute-start(f32[4,8]{1,0:T(4,128)S(1)} %pad_add_fusion), channel_id=1, source_target_pairs={{0,4},{4,0},{8,12},{12,8},{1,5},{5,1},{9,13},{13,9},{2,6},{6,2},{1... | collective-permute-start | bytes 392 | tf_op jit(solution)/shard_map/ppermute | solution.py:226
  4.4 1.6 %collective-permute-done = f32[4,8]{1,0:T(4,128)S(1)} collective-permute-done((f32[4,8]{1,0:T(4,128)S(1)}, f32[4,8]{1,0:T(4,128)S(1)}, u32[]{:S(2)}, u32[]{:S(2)}) %collective-permute-start) | collective-permute-done | bytes 160 | tf_op jit(solution)/shard_map/ppermute | solution.py:226
  6.0 0.1 pad_maximum_fusion
  6.0 3.0 %collective-permute-start.1 = (f32[4,16]{1,0:T(4,128)S(1)}, f32[4,16]{1,0:T(4,128)S(1)}, u32[]{:S(2)}, u32[]{:S(2)}) collective-permute-start(f32[4,16]{1,0:T(4,128)S(1)} %pad_maximum_fusion), channel_id=1, source_target_pairs={{0,8},{4,12},{8,0},{12,4},{1,9},{5,13},{9,1},{13,5},{2,10},{6,14},... | collective-permute-start | bytes 776 | tf_op jit(solution)/shard_map/ppermute | solution.py:226
  9.1 1.6 %collective-permute-done.1 = f32[4,16]{1,0:T(4,128)S(1)} collective-permute-done((f32[4,16]{1,0:T(4,128)S(1)}, f32[4,16]{1,0:T(4,128)S(1)}, u32[]{:S(2)}, u32[]{:S(2)}) %collective-permute-start.1) | collective-permute-done | bytes 288 | tf_op jit(solution)/shard_map/ppermute | solution.py:226
  10.6 0.7 %pad_maximum_fusion.1.refs_0_.refs_5_ = f32[4,32]{1,0:T(4,128)} fusion(f32[4,16]{1,0:T(4,128)S(1)} %collective-permute-done.1, f32[4,8]{1,0:T(4,128)S(1)} %collective-permute-done, f32[4,8]{1,0:T(4,128)S(1)} %pad_add_fusion), kind=kLoop, calls=%fused_computation.3 | loop fusion | flops 256 | bytes 1024 | tf_op jit(solution)/shard_map/concatenate | solution.py:228
  11.3 4.3 %shard_map.136 = f32[8,99,128]{2,1,0:T(8,128)} custom-call(f32[4,32]{1,0:T(4,128)} %pad_maximum_fusion.1.refs_0_.refs_5_, s32[32]{0:T(128)} %refs_1_.2, s32[16]{0:T(128)} %refs_2_.2, s32[2,16]{1,0:T(2,128)} %bitcast.2, s32[16]{0:T(128)} %refs_1_.3, f32[4,32]{1,0:T(4,128)} %pad_maximum_fusion.1.refs_0_.refs_5_, bf16[3,3,16,4096]{3,2,1,0:T(8,128)(2,1)} %refs_6_.2), custom_call_target="tpu_custom_call" | custom-call | tf_op jit(solution)/shard_map/pallas_call | solution.py:255
  15.6 0.9 %slice.25 = f32[4,99,128]{2,1,0:T(8,128)S(1)} slice(f32[8,99,128]{2,1,0:T(8,128)} %shard_map.136), slice={[4:8], [0:99], [0:128]} | slice | bytes 405504 | tf_op jit(solution)/shard_map/slice | solution.py:261
  16.6 0.1 collective-permute-start.2
  16.7 1.5 %collective-permute-done.2 = f32[4,99,128]{2,1,0:T(8,128)S(1)} collective-permute-done((f32[4,99,128]{2,1,0:T(8,128)S(1)}, f32[4,99,128]{2,1,0:T(8,128)S(1)}, u32[]{:S(2)}, u32[]{:S(2)}) %collective-permute-start.2) | collective-permute-done | bytes 202784 | tf_op jit(solution)/shard_map/ppermute | solution.py:226
  18.1 1.0 %slice_add_fusion = f32[4,99,128]{2,1,0:T(8,128)S(1)} fusion(f32[4,99,128]{2,1,0:T(8,128)S(1)} %collective-permute-done.2, f32[8,99,128]{2,1,0:T(8,128)} %shard_map.136), kind=kLoop, calls=%fused_computation | loop fusion | flops 50688 | bytes 608256 | tf_op jit(solution)/shard_map/add | solution.py:259
  19.1 2.0 %collective-permute-start.3 = (f32[2,99,128]{2,1,0:T(8,128)S(1)}, f32[2,99,128]{2,1,0:T(8,128)S(1)}, u32[]{:S(2)}, u32[]{:S(2)}) collective-permute-start(f32[2,99,128]{2,1,0:T(8,128)S(1)} %slice.27), channel_id=1, source_target_pairs={{0,4},{4,0},{8,12},{12,8},{1,5},{5,1},{9,13},{13,9},{2,6},{6,2},{1... | collective-permute-start | bytes 304136 | tf_op jit(solution)/shard_map/ppermute | solution.py:226
  21.1 3.3 %collective-permute-done.3 = f32[2,99,128]{2,1,0:T(8,128)S(1)} collective-permute-done((f32[2,99,128]{2,1,0:T(8,128)S(1)}, f32[2,99,128]{2,1,0:T(8,128)S(1)}, u32[]{:S(2)}, u32[]{:S(2)}) %collective-permute-start.3) | collective-permute-done | bytes 101408 | tf_op jit(solution)/shard_map/ppermute | solution.py:226
  24.4 0.6 %fusion = (f32[1,99,128]{2,1,0:T(8,128)S(1)}, f32[1,99,128]{2,1,0:T(8,128)}) fusion(f32[2,99,128]{2,1,0:T(8,128)S(1)} %slice_add_fusion.1), kind=kLoop, calls=%fused_computation.5 | loop fusion | bytes 202752 | tf_op jit(solution)/shard_map/slice | solution.py:261
  25.0 2.8 %collective-permute-start.4 = (f32[1,99,128]{2,1,0:T(8,128)S(1)}, f32[1,99,128]{2,1,0:T(8,128)S(1)}, u32[]{:S(2)}, u32[]{:S(2)}) collective-permute-start(f32[1,99,128]{2,1,0:T(8,128)S(1)} %get-tuple-element.5), channel_id=1, source_target_pairs={{0,8},{4,12},{8,0},{12,4},{1,9},{5,13},{9,1},{13,5},{2,10},{6,14},... | collective-permute-start | bytes 152072 | tf_op jit(solution)/shard_map/ppermute | solution.py:226
  27.7 2.4 %shard_map.137.refs_2_ = f32[2,64,128]{2,1,0:T(8,128)} custom-call(s32[2,16]{1,0:T(2,128)} %bitcast.3, s32[16]{0:T(128)} %refs_1_.3, f32[16,2,4096]{2,1,0:T(2,128)} %refs_2_.3), custom_call_target="tpu_custom_call" | custom-call | tf_op jit(solution)/shard_map/pallas_call | solution.py:233
  30.1 0.0 collective-permute-done.4.refs_1_
  30.1 0.0 copy-start
  30.1 0.6 %copy-done = f32[1,99,128]{2,1,0:T(8,128)} copy-done((f32[1,99,128]{2,1,0:T(8,128)}, f32[1,99,128]{2,1,0:T(8,128)S(1)}, u32[]{:S(2)}) %copy-start) | copy-done | bytes 50712
  30.7 2.8 %shard_map.138 = f32[3,32,128]{2,1,0:T(8,128)} custom-call(f32[1,99,128]{2,1,0:T(8,128)} %get-tuple-element.6.refs_0_, f32[1,99,128]{2,1,0:T(8,128)} %copy-done, f32[2,64,128]{2,1,0:T(8,128)} %shard_map.137.refs_2_, f32[64,128]{1,0:T(8,128)} %constant.15.clone.refs_3_, f32[64,128]{1,0:T(8,128)} %constant.16.clone.refs_4_, ...), custom_call_target="tpu_custom_call" | custom-call | tf_op jit(solution)/shard_map/pallas_call | solution.py:264
  (2 shorter events, 0.0 us)
Async XLA Ops:
  1.3 4.6 %collective-permute-start = (f32[4,8]{1,0:T(4,128)S(1)}, f32[4,8]{1,0:T(4,128)S(1)}, u32[]{:S(2)}, u32[]{:S(2)}) collective-permute-start(f32[4,8]{1,0:T(4,128)S(1)} %pad_add_fusion), channel_id=1, source_target_pairs={{0,4},{4,0},{8,12},{12,8},{1,5},{5,1},{9,13},{13,9},{2,6},{6,2},{1... | collective-permute-start | bytes 392 | tf_op jit(solution)/shard_map/ppermute | solution.py:226
  6.0 4.6 %collective-permute-start.1 = (f32[4,16]{1,0:T(4,128)S(1)}, f32[4,16]{1,0:T(4,128)S(1)}, u32[]{:S(2)}, u32[]{:S(2)}) collective-permute-start(f32[4,16]{1,0:T(4,128)S(1)} %pad_maximum_fusion), channel_id=1, source_target_pairs={{0,8},{4,12},{8,0},{12,4},{1,9},{5,13},{9,1},{13,5},{2,10},{6,14},... | collective-permute-start | bytes 776 | tf_op jit(solution)/shard_map/ppermute | solution.py:226
  16.6 1.5 %collective-permute-start.2 = (f32[4,99,128]{2,1,0:T(8,128)S(1)}, f32[4,99,128]{2,1,0:T(8,128)S(1)}, u32[]{:S(2)}, u32[]{:S(2)}) collective-permute-start(f32[4,99,128]{2,1,0:T(8,128)S(1)} %slice.25), channel_id=1, source_target_pairs={{0,1},{1,0},{2,3},{3,2},{4,5},{5,4},{6,7},{7,6},{8,9},{9,8},{10,11... | collective-permute-start | bytes 608264 | tf_op jit(solution)/shard_map/ppermute | solution.py:226
  19.1 5.2 %collective-permute-start.3 = (f32[2,99,128]{2,1,0:T(8,128)S(1)}, f32[2,99,128]{2,1,0:T(8,128)S(1)}, u32[]{:S(2)}, u32[]{:S(2)}) collective-permute-start(f32[2,99,128]{2,1,0:T(8,128)S(1)} %slice.27), channel_id=1, source_target_pairs={{0,4},{4,0},{8,12},{12,8},{1,5},{5,1},{9,13},{13,9},{2,6},{6,2},{1... | collective-permute-start | bytes 304136 | tf_op jit(solution)/shard_map/ppermute | solution.py:226
  25.0 5.1 %collective-permute-start.4 = (f32[1,99,128]{2,1,0:T(8,128)S(1)}, f32[1,99,128]{2,1,0:T(8,128)S(1)}, u32[]{:S(2)}, u32[]{:S(2)}) collective-permute-start(f32[1,99,128]{2,1,0:T(8,128)S(1)} %get-tuple-element.5), channel_id=1, source_target_pairs={{0,8},{4,12},{8,0},{12,4},{1,9},{5,13},{9,1},{13,5},{2,10},{6,14},... | collective-permute-start | bytes 152072 | tf_op jit(solution)/shard_map/ppermute | solution.py:226
  30.1 0.6 %copy-start = (f32[1,99,128]{2,1,0:T(8,128)}, f32[1,99,128]{2,1,0:T(8,128)S(1)}, u32[]{:S(2)}) copy-start(f32[1,99,128]{2,1,0:T(8,128)S(1)} %collective-permute-done.4.refs_1_) | copy-start | bytes 152068

commit v3 on v2

--- a/solution.py
+++ b/solution.py
@@ -67,11 +67,11 @@
 
 def partial_kernel(
     slots, delays, ruptures, functions, var_count, cmp_count, single,
-    table_s, slab_s, rup_s, src_s, map_s, table_ref, sgt_ref, out_ref, lhs_ref,
+    slab_s, rup_s, src_s, map_s, table_ref, sgt_ref, kept_ref, sent_ref, lhs_ref, table_s, sem,
 ):
-    comp_half, slab_dev, samples = sgt_ref.shape
-    group = out_ref.shape[0]
-    rows = out_ref.shape[1] // pl.num_programs(1)
+    comp_half, comps, slab_dev, samples = sgt_ref.shape
+    group = 2 * slots if single else 8
+    rows = kept_ref.shape[1] // comps
     points = slab_s.shape[0]
     width = points // slots
     block = 0 if single else pl.program_id(0)
@@ -82,6 +82,13 @@
         my_owner = lax.axis_index("pts")
         my_var = lax.axis_index("var")
         my_core = lax.axis_index("cmp")
+
+        @pl.when(pl.program_id(0) == 0)
+        def _():
+            copy = pltpu.make_async_copy(table_ref, table_s, sem)
+            copy.start()
+            copy.wait()
+
         point = lax.broadcasted_iota(jnp.int32, (1, points), 1)
         rup_of = jnp.zeros((1, points), jnp.int32)
         pos = jnp.zeros((1, points), jnp.int32)
@@ -134,7 +141,7 @@
         lhs_ref[:, :inner] = high
         lhs_ref[:, inner:] = low
 
-    series = sgt_ref[...].reshape(comp_half * slab_dev, samples)
+    series = sgt_ref[:, comp].reshape(comp_half * slab_dev, samples)
     series = jnp.concatenate([series, series], axis=0)
     product = jnp.dot(lhs_ref[...], series, preferred_element_type=jnp.float32)
     tail = jnp.zeros((group, rows * LANES - samples), jnp.float32)
@@ -144,14 +151,35 @@
         if d:
             piece = pltpu.roll(piece, TAU * d, 1)
         total = piece if total is None else total + piece
-    for c in range(pl.num_programs(1)):
+    for c in range(comps):
         @pl.when(comp == c)
         def _():
             for a in range(rows):
-                out_ref[:, c * rows + a, :] = total[:, a * LANES:(a + 1) * LANES]
-
-
-def slip_kernel(var_count, cmp_count, src_s, map_s, slip_hbm, out_ref, slip_ref, sem):
+                store_pieces(block, group, slots, kept_ref, sent_ref, c * rows + a,
+                             total[:, a * LANES:(a + 1) * LANES])
+
+
+def store_pieces(block, group, slots, kept_ref, sent_ref, row, values):
+    if group == 2 * slots:
+        kept_ref[:, row, :] = values[:slots]
+        sent_ref[:, row, :] = values[slots:]
+    else:
+        first = block * group
+
+        @pl.when(first < slots)
+        def _():
+            kept_ref[pl.ds(first, group), row, :] = values
+
+        @pl.when(first >= slots)
+        def _():
+            sent_ref[pl.ds(first - slots, group), row, :] = values
+
+
+def prepare_kernel(
+    var_count, cmp_count, src_s, map_s, slip_hbm, sgt_hbm, out_ref, sgt_ref, slip_ref, sem, sgt_sem
+):
+    load = pltpu.make_async_copy(sgt_hbm, sgt_ref, sgt_sem)
+    load.start()
     blocks = out_ref.shape[1]
     rows_out = blocks // 2
     length = LANES * blocks
@@ -172,6 +200,7 @@
         turned = wide.T
         turned = jnp.concatenate([turned[:blocks], turned[blocks:]], axis=1)
         out_ref[part] = jnp.concatenate([turned, turned], axis=1) * weight
+    load.wait()
 
 
 def dot_pairs(a, b):
@@ -217,10 +246,12 @@
     assert cmp_count == 2 and owners & (owners - 1) == 0
     delays = MOSTP * owners
     rows = -(-(samples + TAU * (delays - 1)) // LANES)
-    group = 8 if targets % 8 == 0 else targets
+    group = 8 if owners % 8 == 0 else targets
+    near = lambda x: pltpu.with_memory_space_constraint(x, pltpu.VMEM)
+    far = lambda x: pltpu.with_memory_space_constraint(x, pltpu.HBM)
     counts = jnp.pad(
-        rup_counts.astype(jnp.float32), ((comp_half, 0), (0, rp_dev - ruptures))
-    )
+        rup_counts, ((comp_half, 0), (0, rp_dev - ruptures))
+    ).astype(jnp.float32)
     table = jnp.pad(moment, ((0, 1), (0, 0))) + counts
     bits = [1 << b for b in range(owners.bit_length() - 1)]
     swap = lambda x, axis, size, bit: lax.ppermute(x, axis, [(i, i ^ bit) for i in range(size)])
@@ -230,43 +261,50 @@
     smem = pl.BlockSpec(memory_space=pltpu.SMEM)
     vmem = pl.BlockSpec(memory_space=pltpu.VMEM)
 
-    slips = pl.pallas_call(
-        lambda *refs: slip_kernel(var_count, cmp_count, *refs),
-        in_specs=[smem, smem, pl.BlockSpec(memory_space=pl.ANY)],
-        out_specs=vmem,
-        out_shape=jax.ShapeDtypeStruct((2, 2 * samples // LANES, LANES), jnp.float32),
-        scratch_shapes=[pltpu.VMEM(slip_spec.shape[1:], jnp.float32), pltpu.SemaphoreType.DMA(())],
-    )(sources, owner_map, slip_spec)
+    slips, series = pl.pallas_call(
+        lambda *refs: prepare_kernel(var_count, cmp_count, *refs),
+        in_specs=[smem, smem] + [pl.BlockSpec(memory_space=pltpu.HBM)] * 2,
+        out_specs=[vmem] * 2,
+        out_shape=[
+            pltpu.VMEM((2, 2 * samples // LANES, LANES), jnp.float32),
+            pltpu.VMEM(sgt.shape, sgt.dtype),
+        ],
+        scratch_shapes=[pltpu.VMEM(slip_spec.shape[1:], jnp.float32)]
+        + [pltpu.SemaphoreType.DMA(())] * 2,
+        compiler_params=pltpu.CompilerParams(vmem_limit_bytes=8 << 20),
+    )(sources, owner_map, far(slip_spec), far(sgt))
 
     partial = pl.pallas_call(
         lambda *refs: partial_kernel(
             owners, delays, ruptures, functions, var_count, cmp_count, targets == group, *refs
         ),
         grid=(targets // group, comps),
-        in_specs=[
-            smem, smem, smem, smem, smem,
-            pl.BlockSpec(table.shape, lambda b, c: (0, 0)),
-            pl.BlockSpec((comp_half, pl.squeezed, slab_dev, samples), lambda b, c: (0, c, 0, 0)),
+        in_specs=[smem] * 4 + [vmem] * 2,
+        out_specs=[vmem] * 2,
+        out_shape=[pltpu.VMEM((owners, comps * rows, LANES), jnp.float32)] * 2,
+        scratch_shapes=[
+            pltpu.VMEM((delays * group, 2 * comp_half * slab_dev), jnp.bfloat16),
+            pltpu.SMEM(table.shape, jnp.float32),
+            pltpu.SemaphoreType.DMA(()),
         ],
-        out_specs=pl.BlockSpec((group, comps * rows, LANES), lambda b, c: (b, 0, 0)),
-        out_shape=jax.ShapeDtypeStruct((targets, comps * rows, LANES), jnp.float32),
-        scratch_shapes=[pltpu.VMEM((delays * group, 2 * comp_half * slab_dev), jnp.bfloat16)],
+        compiler_params=pltpu.CompilerParams(vmem_limit_bytes=40 << 20),
     )
-    kept = partial(table, rp_slab, var_rupture, sources, owner_map, table, sgt)
+    kept, sent = partial(rp_slab, var_rupture, sources, owner_map, near(table), near(series))
     came = None
     for axis, size, bit in [("cmp", cmp_count, 1)] + [("pts", owners, bit) for bit in bits]:
         if came is not None:
-            kept = kept + came
-        middle = kept.shape[0] // 2
-        came = swap(kept[middle:], axis, size, bit)
-        kept = kept[:middle]
+            total = kept + came
+            middle = total.shape[0] // 2
+            kept, sent = total[:middle], total[middle:]
+        came = swap(sent, axis, size, bit)
     tables = transform_tables(comps, rows, samples)
     result = pl.pallas_call(
         lambda *refs: finish_kernel(comps, *refs),
         in_specs=[vmem] * (3 + len(tables)),
         out_specs=vmem,
         out_shape=jax.ShapeDtypeStruct((comps, samples // LANES, LANES), jnp.float32),
-    )(kept, came, slips, *tables)
+        compiler_params=pltpu.CompilerParams(vmem_limit_bytes=24 << 20),
+    )(near(kept), near(came), near(slips), *[near(jnp.asarray(x)) for x in tables])
     return result.reshape(1, comps, samples)
 
 

time: 33.9 us -> 28.9 us (0.85)
  Pallas kernels: 9.51 us -> 6.88 us
  waiting for transfers between devices: 7.85 us -> 10.3 us
  other arithmetic: 3.05 us -> 0.94 us
  starting transfers between devices: 10.9 us -> 9.13 us
  local copies, waits for them, and re-layouts: 2.18 us -> 1.4 us
    ppermute x5, waiting for transfers between devices: 7.85 us -> 10.3 us  [per_device(): lax.ppermute(x, axis, [(i, i ^ bit) for i in range(size)])]
    ppermute x5, starting transfers between devices: 10.9 us -> 9.13 us  [per_device(): lax.ppermute(x, axis, [(i, i ^ bit) for i in range(size)])]
    slice x3 -> x2, local copies, waits for them, and re-layouts: 1.58 us -> 0.02 us  [per_device(): kept, sent = (total[:middle], total[middle:])]
    pallas_call x2, Pallas kernels: 6.7 us -> 5.29 us  [the longest x1 3.36 us: per_device(): partial(rp_slab, var_rupture, sources, owner_map, near(table), near(series))]
    pallas_call x1, Pallas kernels: 2.82 us -> 1.59 us  [per_device(): pl.pallas_call(lambda *refs: finish_kernel(comps, *refs), in_specs=[vmem]...]
    add x2, other arithmetic: 0.98 us -> 0.04 us  [per_device(): total = kept + came]
    unnamed x2 -> x22, local copies, waits for them, and re-layouts: 0.6 us -> 1.39 us
    convert_element_type x1 -> x0, other arithmetic: 0.66 us -> none  [per_device(): rup_counts.astype(jnp.float32)]
where the time goes in v3:
time: 28.9 us; the launch traced here: 28.7 us
  waiting for transfers between devices  10.3 us (36%)
  starting transfers between devices  9.13 us (32%)
  Pallas kernels  6.88 us (24%)
  local copies, waits for them, and re-layouts  1.4 us (5%)
  other arithmetic  0.94 us (3%)
    ppermute x5, waiting for transfers between devices, per_device(): lax.ppermute(x, axis, [(i, i ^ bit) for i in range(size)])  10.3 us
    ppermute x5, starting transfers between devices, per_device(): lax.ppermute(x, axis, [(i, i ^ bit) for i in range(size)])  9.13 us
    pallas_call x1, Pallas kernels, per_device(): partial(rp_slab, var_rupture, sources, owner_map, near(table), near(series))  3.36 us
    pallas_call x1, Pallas kernels, per_device(): pl.pallas_call(lambda *refs: prepare_kernel(var_count, cmp_count, *refs),...  1.93 us
    pallas_call x1, Pallas kernels, per_device(): pl.pallas_call(lambda *refs: finish_kernel(comps, *refs), in_specs=[vmem]...  1.59 us
    unnamed x22, local copies, waits for them, and re-layouts  1.39 us
    add x1, other arithmetic, per_device(): table = jnp.pad(moment, ((0, 1), (0, 0))) + counts  0.75 us
  transfers between devices with their start and end apart: 5, of which 4 were waited for; matrix products, arithmetic and copies ran while one was open for 0% of the time, Pallas kernels for 7%

profile of v3, /device:TPU:0, one launch (start us, length us, event | category | flops | bytes accessed | tf_op | source)
XLA Modules:
  0.0 28.7 jit_solution(12754247196701100216)
XLA Ops:
  0.0 0.0 copy-start.7
  0.0 0.0 copy-start.10
  0.0 0.0 copy-start.9
  0.0 0.7 %convert_add_fusion = f32[4,8]{1,0:T(4,128)S(1)} fusion(s32[1,6]{1,0:T(1,128)} %param.18, f32[3,8]{1,0:T(4,128)} %param.15), kind=kLoop, calls=%fused_computation.3 | loop fusion | flops 64 | bytes 248 | tf_op jit(solution)/shard_map/add | solution.py:255
  0.8 3.1 %collective-permute-start = (f32[4,8]{1,0:T(4,128)S(1)}, f32[4,8]{1,0:T(4,128)S(1)}, u32[]{:S(2)}, u32[]{:S(2)}) collective-permute-start(f32[4,8]{1,0:T(4,128)S(1)} %convert_add_fusion), channel_id=1, source_target_pairs={{0,4},{4,0},{8,12},{12,8},{1,5},{5,1},{9,13},{13,9},{2,6},{6,2},{1... | collective-permute-start | bytes 392 | tf_op jit(solution)/shard_map/ppermute | solution.py:257
  3.8 1.6 %collective-permute-done = f32[4,8]{1,0:T(4,128)S(1)} collective-permute-done((f32[4,8]{1,0:T(4,128)S(1)}, f32[4,8]{1,0:T(4,128)S(1)}, u32[]{:S(2)}, u32[]{:S(2)}) %collective-permute-start) | collective-permute-done | bytes 160 | tf_op jit(solution)/shard_map/ppermute | solution.py:257
  5.4 0.1 pad_maximum_fusion
  5.5 3.0 %collective-permute-start.1 = (f32[4,16]{1,0:T(4,128)S(1)}, f32[4,16]{1,0:T(4,128)S(1)}, u32[]{:S(2)}, u32[]{:S(2)}) collective-permute-start(f32[4,16]{1,0:T(4,128)S(1)} %pad_maximum_fusion), channel_id=1, source_target_pairs={{0,8},{4,12},{8,0},{12,4},{1,9},{5,13},{9,1},{13,5},{2,10},{6,14},... | collective-permute-start | bytes 776 | tf_op jit(solution)/shard_map/ppermute | solution.py:257
  8.5 0.0 copy-start.6
  8.5 0.7 %copy-done.6 = s32[16,2]{0,1:T(2,128)S(1)} copy-done((s32[16,2]{0,1:T(2,128)S(1)}, s32[16,2]{0,1:T(2,128)}, u32[]{:S(2)}) %copy-start.6) | copy-done | bytes 152
  9.2 0.0 copy-start.8
  9.2 0.7 %copy-done.8 = s32[16]{0:T(128)S(1)} copy-done((s32[16]{0:T(128)S(1)}, s32[16]{0:T(128)}, u32[]{:S(2)}) %copy-start.8) | copy-done | bytes 88
  9.9 1.9 %shard_map.136 = (f32[2,64,128]{2,1,0:T(8,128)S(1)}, bf16[3,3,16,4096]{3,2,1,0:T(8,128)(2,1)S(1)}) custom-call(s32[2,16]{1,0:T(2,128)S(1)} %bitcast.2, s32[16]{0:T(128)S(1)} %copy-done.8, f32[16,2,4096]{2,1,0:T(2,128)} %refs_2_.1, bf16[3,3,16,4096]{3,2,1,0:T(8,128)(2,1)} %refs_3_.3), custom_call_target="tpu_custom_call" | custom-call | tf_op jit(solution)/shard_map/pallas_call | solution.py:264
  11.8 0.0 collective-permute-done.1
  11.8 0.1 pad_maximum_fusion.1.refs_4_
  11.9 0.0 copy-done.7
  11.9 0.0 copy-done.10
  11.9 0.0 copy-done.9
  11.9 0.0 copy-start
  11.9 0.0 copy-start.1
  11.9 0.0 copy-start.2
  11.9 0.0 copy-start.3
  11.9 0.0 copy-start.4
  12.0 0.0 copy-start.5
  12.0 3.4 %shard_map.137 = (f32[4,99,128]{2,1,0:T(8,128)S(1)}, f32[4,99,128]{2,1,0:T(8,128)S(1)}) custom-call(s32[32]{0:T(128)S(1)} %copy-done.9, s32[16]{0:T(128)S(1)} %copy-done.10, s32[2,16]{1,0:T(2,128)S(1)} %bitcast.3, s32[16]{0:T(128)S(1)} %copy-done.8, f32[4,32]{1,0:T(4,128)S(1)} %pad_maximum_fusion.1.refs_4_, bf16[3,3,16,4096]{3,2,1,0:T(8,128)(2,1)S(1)} %get-tuple-element.9.refs_5_), custom_call_target="tpu_custom_call" | custom-call | tf_op jit(solution)/shard_map/pallas_call | solution.py:292
  15.3 0.1 collective-permute-start.2
  15.4 1.5 %collective-permute-done.2 = f32[4,99,128]{2,1,0:T(8,128)S(1)} collective-permute-done((f32[4,99,128]{2,1,0:T(8,128)S(1)}, f32[4,99,128]{2,1,0:T(8,128)S(1)}, u32[]{:S(2)}, u32[]{:S(2)}) %collective-permute-start.2) | collective-permute-done | bytes 202784 | tf_op jit(solution)/shard_map/ppermute | solution.py:257
  16.9 1.7 %collective-permute-start.3 = (f32[2,99,128]{2,1,0:T(8,128)S(1)}, f32[2,99,128]{2,1,0:T(8,128)S(1)}, u32[]{:S(2)}, u32[]{:S(2)}) collective-permute-start(f32[2,99,128]{2,1,0:T(8,128)S(1)} %slice.17), channel_id=1, source_target_pairs={{0,4},{4,0},{8,12},{12,8},{1,5},{5,1},{9,13},{13,9},{2,6},{6,2},{1... | collective-permute-start | bytes 304136 | tf_op jit(solution)/shard_map/ppermute | solution.py:257
  18.6 3.4 %collective-permute-done.3 = f32[2,99,128]{2,1,0:T(8,128)S(1)} collective-permute-done((f32[2,99,128]{2,1,0:T(8,128)S(1)}, f32[2,99,128]{2,1,0:T(8,128)S(1)}, u32[]{:S(2)}, u32[]{:S(2)}) %collective-permute-start.3) | collective-permute-done | bytes 101408 | tf_op jit(solution)/shard_map/ppermute | solution.py:257
  22.0 1.3 %collective-permute-start.4 = (f32[1,99,128]{2,1,0:T(8,128)S(1)}, f32[1,99,128]{2,1,0:T(8,128)S(1)}, u32[]{:S(2)}, u32[]{:S(2)}) collective-permute-start(f32[1,99,128]{2,1,0:T(8,128)S(1)} %get-tuple-element.13), channel_id=1, source_target_pairs={{0,8},{4,12},{8,0},{12,4},{1,9},{5,13},{9,1},{13,5},{2,10},{6,14},... | collective-permute-start | bytes 152072 | tf_op jit(solution)/shard_map/ppermute | solution.py:257
  23.3 3.8 %collective-permute-done.4.refs_1_ = f32[1,99,128]{2,1,0:T(8,128)S(1)} collective-permute-done((f32[1,99,128]{2,1,0:T(8,128)S(1)}, f32[1,99,128]{2,1,0:T(8,128)S(1)}, u32[]{:S(2)}, u32[]{:S(2)}) %collective-permute-start.4) | collective-permute-done | bytes 50720 | tf_op jit(solution)/shard_map/ppermute | solution.py:257
  27.1 0.0 copy-done
  27.1 0.0 copy-done.1
  27.1 0.0 copy-done.2
  27.1 0.0 copy-done.3
  27.1 0.0 copy-done.4
  27.1 0.0 copy-done.5
  27.2 1.6 %shard_map.138 = f32[3,32,128]{2,1,0:T(8,128)} custom-call(f32[1,99,128]{2,1,0:T(8,128)S(1)} %get-tuple-element.14.refs_0_, f32[1,99,128]{2,1,0:T(8,128)S(1)} %collective-permute-done.4.refs_1_, f32[2,64,128]{2,1,0:T(8,128)S(1)} %get-tuple-element.12.refs_2_, f32[64,128]{1,0:T(8,128)S(1)} %copy-done.4, f32[64,128]{1,0:T(8,128)S(1)} %copy-done.3, ...), custom_call_target="tpu_custom_call" | custom-call | tf_op jit(solution)/shard_map/pallas_call | solution.py:301
  (4 shorter events, 0.1 us)
Async XLA Ops:
  0.0 11.9 %copy-start.7 = (s32[16,2]{0,1:T(2,128)S(1)}, s32[16,2]{0,1:T(2,128)}, u32[]{:S(2)}) copy-start(s32[16,2]{0,1:T(2,128)} %param.20) | copy-start | bytes 388
  0.0 11.9 %copy-start.10 = (s32[16]{0:T(128)S(1)}, s32[16]{0:T(128)}, u32[]{:S(2)}) copy-start(s32[16]{0:T(128)} %refs_1_.3) | copy-start | bytes 196
  0.0 11.9 %copy-start.9 = (s32[32]{0:T(128)S(1)}, s32[32]{0:T(128)}, u32[]{:S(2)}) copy-start(s32[32]{0:T(128)} %refs_0_.1) | copy-start | bytes 388
  0.8 4.7 %collective-permute-start = (f32[4,8]{1,0:T(4,128)S(1)}, f32[4,8]{1,0:T(4,128)S(1)}, u32[]{:S(2)}, u32[]{:S(2)}) collective-permute-start(f32[4,8]{1,0:T(4,128)S(1)} %convert_add_fusion), channel_id=1, source_target_pairs={{0,4},{4,0},{8,12},{12,8},{1,5},{5,1},{9,13},{13,9},{2,6},{6,2},{1... | collective-permute-start | bytes 392 | tf_op jit(solution)/shard_map/ppermute | solution.py:257
  5.5 6.3 %collective-permute-start.1 = (f32[4,16]{1,0:T(4,128)S(1)}, f32[4,16]{1,0:T(4,128)S(1)}, u32[]{:S(2)}, u32[]{:S(2)}) collective-permute-start(f32[4,16]{1,0:T(4,128)S(1)} %pad_maximum_fusion), channel_id=1, source_target_pairs={{0,8},{4,12},{8,0},{12,4},{1,9},{5,13},{9,1},{13,5},{2,10},{6,14},... | collective-permute-start | bytes 776 | tf_op jit(solution)/shard_map/ppermute | solution.py:257
  8.5 0.7 %copy-start.6 = (s32[16,2]{0,1:T(2,128)S(1)}, s32[16,2]{0,1:T(2,128)}, u32[]{:S(2)}) copy-start(s32[16,2]{0,1:T(2,128)} %param.20) | copy-start | bytes 388
  9.2 0.7 %copy-start.8 = (s32[16]{0:T(128)S(1)}, s32[16]{0:T(128)}, u32[]{:S(2)}) copy-start(s32[16]{0:T(128)} %refs_3_.4) | copy-start | bytes 196
  11.9 15.2 %copy-start = (bf16[2,256,256]{2,1,0:T(8,128)(2,1)S(1)}, bf16[2,256,256]{2,1,0:T(8,128)(2,1)}, u32[]{:S(2)}) copy-start(bf16[2,256,256]{2,1,0:T(8,128)(2,1)} %constant.19.clone.refs_6_) | copy-start | bytes 786436
  11.9 15.2 %copy-start.1 = (bf16[2,384,99]{2,1,0:T(8,128)(2,1)S(1)}, bf16[2,384,99]{2,1,0:T(8,128)(2,1)}, u32[]{:S(2)}) copy-start(bf16[2,384,99]{2,1,0:T(8,128)(2,1)} %constant.18.clone.refs_5_) | copy-start | bytes 456196
  11.9 15.2 %copy-start.2 = (bf16[2,128,256]{2,1,0:T(8,128)(2,1)S(1)}, bf16[2,128,256]{2,1,0:T(8,128)(2,1)}, u32[]{:S(2)}) copy-start(bf16[2,128,256]{2,1,0:T(8,128)(2,1)} %constant.20.clone.refs_7_) | copy-start | bytes 393220
  11.9 15.2 %copy-start.3 = (f32[64,128]{1,0:T(8,128)S(1)}, f32[64,128]{1,0:T(8,128)}, u32[]{:S(2)}) copy-start(f32[64,128]{1,0:T(8,128)} %constant.17.clone.refs_4_) | copy-start | bytes 98308
  11.9 15.2 %copy-start.4 = (f32[64,128]{1,0:T(8,128)S(1)}, f32[64,128]{1,0:T(8,128)}, u32[]{:S(2)}) copy-start(f32[64,128]{1,0:T(8,128)} %constant.16.clone.refs_3_) | copy-start | bytes 98308
  12.0 15.2 %copy-start.5 = (bf16[2,32,128]{2,1,0:T(8,128)(2,1)S(1)}, bf16[2,32,128]{2,1,0:T(8,128)(2,1)}, u32[]{:S(2)}) copy-start(bf16[2,32,128]{2,1,0:T(8,128)(2,1)} %constant.21.clone.refs_8_) | copy-start | bytes 49156
  15.3 1.5 %collective-permute-start.2 = (f32[4,99,128]{2,1,0:T(8,128)S(1)}, f32[4,99,128]{2,1,0:T(8,128)S(1)}, u32[]{:S(2)}, u32[]{:S(2)}) collective-permute-start(f32[4,99,128]{2,1,0:T(8,128)S(1)} %get-tuple-element.11), channel_id=1, source_target_pairs={{0,1},{1,0},{2,3},{3,2},{4,5},{5,4},{6,7},{7,6},{8,9},{9,8},{10,11... | collective-permute-start | bytes 608264 | tf_op jit(solution)/shard_map/ppermute | solution.py:257
  16.9 5.1 %collective-permute-start.3 = (f32[2,99,128]{2,1,0:T(8,128)S(1)}, f32[2,99,128]{2,1,0:T(8,128)S(1)}, u32[]{:S(2)}, u32[]{:S(2)}) collective-permute-start(f32[2,99,128]{2,1,0:T(8,128)S(1)} %slice.17), channel_id=1, source_target_pairs={{0,4},{4,0},{8,12},{12,8},{1,5},{5,1},{9,13},{13,9},{2,6},{6,2},{1... | collective-permute-start | bytes 304136 | tf_op jit(solution)/shard_map/ppermute | solution.py:257
  22.0 5.1 %collective-permute-start.4 = (f32[1,99,128]{2,1,0:T(8,128)S(1)}, f32[1,99,128]{2,1,0:T(8,128)S(1)}, u32[]{:S(2)}, u32[]{:S(2)}) collective-permute-start(f32[1,99,128]{2,1,0:T(8,128)S(1)} %get-tuple-element.13), channel_id=1, source_target_pairs={{0,8},{4,12},{8,0},{12,4},{1,9},{5,13},{9,1},{13,5},{2,10},{6,14},... | collective-permute-start | bytes 152072 | tf_op jit(solution)/shard_map/ppermute | solution.py:257
